TPU v7x, 32 devices: a whole 2x2x4 slice. The times are simulated.
32 devices in a mesh: grp: 2 (over x), bus: 16 (over z, y, core).
Axes of the slice: x: 2, y: 2, z: 4, core: 2. Of those that a mesh axis runs over, the one named last changes fastest.
Arguments:
- series: bfloat16 [32, 2048, 1024], P(('grp', 'bus')), parts along dimension 0, may hold values from -6 to 6
- hour_ids: int32 [32], P(('grp', 'bus')), parts along dimension 0, may hold values from 0 to 23
- hour_table: bfloat16 [24, 1024], replicated, may hold values from -3 to 3
- norm_gain: float32 [1024], replicated, may hold values from 0.1 to 1.9
- bus_order: int32 [4096], P('grp'), parts along dimension 0, may hold values from 0 to 2047, each once
- w_query: bfloat16 [1024, 512], replicated, may hold values from -0.1875 to 0.1875
- w_key: bfloat16 [1024, 512], replicated, may hold values from -0.1875 to 0.1875
- w_value: bfloat16 [1024, 512], replicated, may hold values from -0.1875 to 0.1875
- score_scale: float32 [8], replicated, may hold values from 0.5 to 10, as said below
- neighbors: int32 [32, 3], P('grp'), parts along dimension 0, may hold values from -1 to 15, as said below
- grad_out: bfloat16 [32, 2048, 512], P('grp', 'bus'), parts along dimension 0, may hold values from -6 to 6
Outputs:
- key_grad: bfloat16 [32, 2048, 512], P('grp', 'bus'), parts along dimension 0
- value_grad: bfloat16 [32, 2048, 512], P('grp', 'bus'), parts along dimension 0
There are 2 independent parts, one for each index of `grp`. A program takes and returns all parts, laid end to end along the dimension named above; an argument that names none is the same for every part. Nothing has to cross between parts.
Inputs may be any that keep to these rules, and one draw needn't show every extreme that they name: `neighbors`: row b lists the key blocks read by query block b: entry 0 is b - 1 or -1, entry 1 is b, entry 2 is b + 1 or -1; -1 marks a block not read, and stands in entry 0 of row 0 and entry 2 of row 15. `score_scale`: positive temperatures of the heads.
All inputs are finite; a program needn't handle non-finite values.
Results may differ from a plain program's by a relative error of at most 0.018.
The roundings to bfloat16 on the way count: a program that leaves them out, or rounds other values in their place, can miss the bound.
Values may be sent and summed in bfloat16 or wider, within the bound.
No kernel may reach another device: no remote copies, remote signals or barrier semaphores. Data moves between devices by JAX's collectives and lax.ppermute only.
A program may use at most 256 MiB of HBM per device.

v0:
```python
import math
import jax
import jax.numpy as jnp
from jax import lax
from jax.sharding import PartitionSpec as P

EPSILON = 1e-05
NEG_FILL = -1e30


def with_halo(shard, sides, width):
    for axis, dim in sides:
        devices, length = (lax.axis_size(axis), shard.shape[dim])
        up = [(i, (i + 1) % devices) for i in range(devices - 1)]
        down = [(j, i) for i, j in up]
        last = lax.slice_in_dim(shard, length - width, length, axis=dim)
        leading = lax.slice_in_dim(shard, 0, width, axis=dim)
        before = lax.ppermute(last, axis, up)
        after = lax.ppermute(leading, axis, down)
        shard = jnp.concatenate([before, shard, after], axis=dim)
    return shard


def from_behind(value, axis, steps):
    count = lax.axis_size(axis)
    leading, last = (max(0, -steps), min(count, count - steps))
    return lax.ppermute(value, axis, [(source, source + steps) for source in range(leading, last)])


def split_heads(array, head_count):
    return array.reshape(array.shape[0], array.shape[1], head_count, array.shape[2] // head_count)


def over_groups(step_fn, arrays, group_size):
    stacked = tuple(
        (
            item.reshape((item.shape[0] // group_size, group_size) + item.shape[1:])
            for item in arrays
        )
    )
    results = lax.map(lambda pieces: step_fn(*pieces), stacked)
    return tuple((item.reshape((-1,) + item.shape[2:]) for item in results))


def reader_terms(queries, key_tiles, value_tiles, grad_rows, colvalid, head_scale):
    scores = (
        jnp.einsum("sihd,sjhd->shij", queries, key_tiles, preferred_element_type=jnp.float32)
        * head_scale[None, :, None, None]
    )
    scores = jnp.where(colvalid[None, None, None, :], scores, NEG_FILL)
    row_max = jnp.max(scores, axis=-1)
    log_total = row_max + jnp.log(jnp.sum(jnp.exp(scores - row_max[..., None]), axis=-1))
    weights = jnp.exp(scores - log_total[..., None])
    weights_b = weights.astype(jnp.bfloat16)
    attended = jnp.einsum(
        "shij,sjhd->sihd", weights_b, value_tiles, preferred_element_type=jnp.float32
    ).astype(jnp.bfloat16)
    row_dot = jnp.einsum("sihd,sihd->shi", grad_rows, attended, preferred_element_type=jnp.float32)
    dweights = jnp.einsum(
        "sihd,sjhd->shij", grad_rows, value_tiles, preferred_element_type=jnp.float32
    )
    dscores = (weights * (dweights - row_dot[..., None]) * head_scale[None, :, None, None]).astype(
        jnp.bfloat16
    )
    value_part = jnp.einsum(
        "shij,sihd->sjhd", weights_b, grad_rows, preferred_element_type=jnp.float32
    )
    key_part = jnp.einsum("shij,sihd->sjhd", dscores, queries, preferred_element_type=jnp.float32)
    return (log_total, row_dot, key_part.astype(jnp.bfloat16), value_part.astype(jnp.bfloat16))


def on_device(
    series,
    hour_ids,
    hour_table,
    norm_gain,
    bus_order,
    w_query,
    w_key,
    w_value,
    score_scale,
    neighbors,
    grad_out,
):
    head_count = score_scale.shape[0]
    snap_count = grad_out.shape[0]
    block_rows = grad_out.shape[1]
    feat_width = grad_out.shape[2]
    head_dim = feat_width // head_count
    ordered = jnp.take(series, bus_order, axis=1)
    onehot = (
        hour_ids[:, None] == jnp.arange(hour_table.shape[0], dtype=jnp.int32)[None, :]
    ).astype(jnp.bfloat16)
    hour_rows = jnp.dot(onehot, hour_table, preferred_element_type=jnp.float32)
    mixed = ordered.astype(jnp.float32) + hour_rows[:, None, :]
    normed = (
        mixed * lax.rsqrt(jnp.mean(mixed * mixed, axis=-1, keepdims=True) + EPSILON) * norm_gain
    ).astype(jnp.bfloat16)
    arrived = lax.all_to_all(normed, "bus", split_axis=1, concat_axis=0, tiled=True)
    flat_rows = arrived.reshape(-1, arrived.shape[2])
    queries, key_rows, value_rows = [
        jnp.dot(flat_rows, weight, preferred_element_type=jnp.float32)
        .astype(jnp.bfloat16)
        .reshape(snap_count, block_rows, feat_width)
        for weight in (w_query, w_key, w_value)
    ]
    dev_index = lax.axis_index("bus")
    own_row = lax.dynamic_slice_in_dim(neighbors, dev_index, 1, 0)[0]
    colvalid = jnp.repeat(own_row >= 0, block_rows)
    head_scale = score_scale / math.sqrt(head_dim)
    group_size = math.gcd(snap_count, max(1, 512 // block_rows))
    kv_tiles = with_halo(jnp.stack([key_rows, value_rows]), (("bus", 2),), block_rows)
    query_heads = split_heads(queries, head_count)
    grad_heads = split_heads(grad_out, head_count)
    key_heads = split_heads(kv_tiles[0], head_count)
    value_heads = split_heads(kv_tiles[1], head_count)

    def full_step(query_part, key_part, value_part, grad_part):
        return reader_terms(query_part, key_part, value_part, grad_part, colvalid, head_scale)

    log_total, row_dot, key_part, value_part = over_groups(
        full_step, (query_heads, key_heads, value_heads, grad_heads), group_size
    )
    partials = jnp.stack(
        [
            key_part.reshape(snap_count, 3 * block_rows, feat_width),
            value_part.reshape(snap_count, 3 * block_rows, feat_width),
        ]
    )
    from_upper = from_behind(partials[:, :, :block_rows], "bus", -1)
    from_lower = from_behind(partials[:, :, 2 * block_rows :], "bus", 1)
    summed = (
        partials[:, :, block_rows : 2 * block_rows].astype(jnp.float32)
        + from_lower.astype(jnp.float32)
        + from_upper.astype(jnp.float32)
    )
    key_grad = summed[0].astype(jnp.bfloat16)
    value_grad = summed[1].astype(jnp.bfloat16)
    return (key_grad, value_grad)


def solution(mesh):
    return jax.shard_map(
        on_device,
        mesh=mesh,
        in_specs=(
            P(("grp", "bus"), None, None),
            P(("grp", "bus")),
            P(),
            P(),
            P("grp"),
            P(),
            P(),
            P(),
            P(),
            P("grp", None),
            P("grp", "bus", None),
        ),
        out_specs=(P("grp", "bus", None), P("grp", "bus", None)),
        check_vma=False,
    )
```

profile of v0, /device:TPU:12, one launch (start us, length us, event | category | flops | bytes accessed | tf_op | source)
XLA Modules:
  0.0 511.9 jit_solution(18104541909109588138)
XLA Ops:
  2.8 13.7 %gather_fusion = bf16[2048,1024]{1,0:T(8,128)(2,1)} fusion(bf16[2048,1024]{1,0:T(8,128)(2,1)} %bitcast.128, s32[2048]{0:T(1024)S(1)} %fusion.71), kind=kCustom, calls=%fused_computation | custom fusion | bytes 8396800 | tf_op jit(solution)/shard_map/jit(_take)/gather | solution.py:90
  16.6 3.6 multiply_reduce_fusion
  22.0 28.7 %copy.65 = bf16[1,2048,1024]{2,0,1:T(2,128)(2,1)} copy(bf16[1,2048,1024]{2,1,0:T(8,128)(2,1)S(1)} %multiply_convert_fusion.6) | data formatting | bytes 8388608 | tf_op jit(solution)/shard_map/convert_element_type | solution.py:98
  51.3 25.9 %reduce.5 = bf16[2048,1024]{1,0:T(8,128)(2,1)} reduce(bf16[2048,1,1024]{2,1,0:T(2,128)(2,1)} %bitcast.129, bf16[]{:T(256)} %broadcast.169), dimensions={1}, to_apply=%bitcast.102.reduce_sub_computation | reduce | bytes 8388610
  77.2 11.4 %reshape.223 = bf16[16,2,65536]{2,1,0:T(2,128)(2,1)} reshape(bf16[2048,1024]{1,0:T(8,128)(2,1)} %reduce.5) | data formatting | bytes 8388608
  88.6 98.4 %all_to_all.4 = bf16[16,2,65536]{2,1,0:T(2,128)(2,1)} all-to-all(bf16[16,2,65536]{2,1,0:T(2,128)(2,1)} %reshape.223), channel_id=1, replica_groups=mesh['grp'=2,'bus'=16] {'bus'}, dimensions={0} | all-to-all | bytes 8388608 | tf_op jit(solution)/shard_map/all_to_all | solution.py:99
  187.0 12.3 %reshape.224 = bf16[2048,1,1024]{2,1,0:T(2,128)(2,1)} reshape(bf16[16,2,65536]{2,1,0:T(2,128)(2,1)} %all_to_all.4) | data formatting | bytes 8388608
  199.3 7.1 %fusion.65 = bf16[2048,512]{1,0:T(8,128)(2,1)} fusion(bf16[1024,512]{1,0:T(8,128)(2,1)S(1)} %copy-done, bf16[1,2048,1024]{2,0,1:T(2,128)(2,1)} %bitcast.135), kind=kOutput, calls=%fused_computation.64 | convolution fusion | flops 2148532224 | bytes 7340032 | tf_op jit(solution)/shard_map/dot_general | solution.py:102
  209.5 7.3 %fusion.68 = bf16[2048,512]{1,0:T(8,128)(2,1)} fusion(bf16[1024,512]{1,0:T(8,128)(2,1)} %param.20, bf16[1,2048,1024]{2,0,1:T(2,128)(2,1)} %bitcast.136), kind=kOutput, calls=%fused_computation.65 | convolution fusion | flops 2148532224 | bytes 7340032 | tf_op jit(solution)/shard_map/dot_general | solution.py:102
  216.8 3.9 copy.37
  220.7 3.9 pad_maximum_fusion.2
  226.9 3.6 collective-permute-start.1
  230.5 3.9 copy.38
  234.6 7.3 %fusion.62 = bf16[2048,512]{1,0:T(8,128)(2,1)} fusion(bf16[1024,512]{1,0:T(8,128)(2,1)} %param.18, bf16[1,2048,1024]{2,0,1:T(2,128)(2,1)} %bitcast.137), kind=kOutput, calls=%fused_computation.63 | convolution fusion | flops 2148532224 | bytes 7340032 | tf_op jit(solution)/shard_map/dot_general | solution.py:102
  241.9 6.1 %reshape.221 = bf16[4,4,128,8,64]{4,3,2,1,0:T(8,128)(2,1)} reshape(bf16[2048,512]{1,0:T(8,128)(2,1)} %fusion.62) | data formatting | bytes 4194304 | tf_op jit(solution)/shard_map/reshape;reshape;reshape | solution.py:37
  248.1 5.1 copy.39
  253.1 66.6 %collective-permute-done = bf16[2,16,128,512]{2,3,1,0:T(8,128)(2,1)} collective-permute-done((bf16[2,16,128,512]{2,3,1,0:T(8,128)(2,1)}, bf16[2,16,128,512]{2,3,1,0:T(8,128)(2,1)}, u32[]{:S(2)}, u32[]{:S(2)}) %collective-permute-start) | collective-permute-done | bytes 4194336 | tf_op jit(solution)/shard_map/ppermute | solution.py:18
  319.7 6.3 %pad_maximum_fusion = bf16[2,16,384,512]{2,3,1,0:T(8,128)(2,1)S(1)} fusion(bf16[2,16,128,512]{2,3,1,0:T(8,128)(2,1)} %collective-permute-done.1, bf16[1,16,128,512]{2,3,1,0:T(8,128)(2,1)} %copy.37, bf16[1,16,128,512]{2,3,1,0:T(8,128)(2,1)S(1)} %copy.36, bf16[2,16,128,512]{2,3,1,0:T(8,128)(2,1)} %collective-permute-done), kind=kLoop, calls=%fused_computation.47 | loop fusion | flops 50331648 | bytes 25165824 | tf_op jit(solution)/shard_map/concatenate | solution.py:20
  326.1 5.9 %fusion.81 = (bf16[1,16,384,512]{2,3,1,0:T(8,128)(2,1)}, bf16[1,16,384,512]{2,3,1,0:T(8,128)(2,1)}) fusion(bf16[2,16,384,512]{2,3,1,0:T(8,128)(2,1)S(1)} %pad_maximum_fusion), kind=kLoop, calls=%fused_computation.83 | loop fusion | bytes 25165824 | tf_op jit(solution)/shard_map/slice | solution.py:116
  332.0 70.7 %while.13 = (s32[]{:T(128)}, bf16[4,4,384,8,64]{2,4,3,1,0:T(8,128)(2,1)}, bf16[4,4,384,8,64]{2,4,3,1,0:T(8,128)(2,1)}, bf16[4,4,128,8,64]{2,4,3,1,0:T(8,128)(2,1...) while((s32[]{:T(128)}, ...), condition=%wide.region_4.5_spmd.clone, body=%wide.region_1.0_spmd.clone.sunk | while | flops 1044111360 | bytes 75687264 | solution.py:41
  340.1 3.4 fusion.103
  343.5 6.2 %bitcast_dynamic-update-slice_fusion.4 = bf16[4,4,384,8,64]{2,4,3,1,0:T(8,128)(2,1)} fusion(bf16[4,4,384,8,64]{2,4,3,1,0:T(8,128)(2,1)} %get-tuple-element.211, s32[]{:T(128)} %get-tuple-element.210, f32[4,8,128,384]{3,2,1,0:T(8,128)} %copy-done.2, f32[4,8,128]{2,1,0:T(8,128)S(1)} %fusion.103, f32[4,8,128]{2,1,0:T(8,128)S(1)} %log_add_fusion.2, ...), kind=kOutput, calls=%fused_computation.14.clone.1 | convolution fusion | flops 414449664 | bytes 10521600 | tf_op jit(solution)/shard_map/while/body/eval_jaxpr/shij,sihd->sjhd/dot_general | solution.py:68
  357.7 3.4 fusion.103
  361.2 6.2 %bitcast_dynamic-update-slice_fusion.4 = bf16[4,4,384,8,64]{2,4,3,1,0:T(8,128)(2,1)} fusion(bf16[4,4,384,8,64]{2,4,3,1,0:T(8,128)(2,1)} %get-tuple-element.211, s32[]{:T(128)} %get-tuple-element.210, f32[4,8,128,384]{3,2,1,0:T(8,128)} %copy-done.2, f32[4,8,128]{2,1,0:T(8,128)S(1)} %fusion.103, f32[4,8,128]{2,1,0:T(8,128)S(1)} %log_add_fusion.2, ...), kind=kOutput, calls=%fused_computation.14.clone.1 | convolution fusion | flops 414449664 | bytes 10521600 | tf_op jit(solution)/shard_map/while/body/eval_jaxpr/shij,sihd->sjhd/dot_general | solution.py:68
  375.5 3.4 fusion.103
  378.9 6.2 %bitcast_dynamic-update-slice_fusion.4 = bf16[4,4,384,8,64]{2,4,3,1,0:T(8,128)(2,1)} fusion(bf16[4,4,384,8,64]{2,4,3,1,0:T(8,128)(2,1)} %get-tuple-element.211, s32[]{:T(128)} %get-tuple-element.210, f32[4,8,128,384]{3,2,1,0:T(8,128)} %copy-done.2, f32[4,8,128]{2,1,0:T(8,128)S(1)} %fusion.103, f32[4,8,128]{2,1,0:T(8,128)S(1)} %log_add_fusion.2, ...), kind=kOutput, calls=%fused_computation.14.clone.1 | convolution fusion | flops 414449664 | bytes 10521600 | tf_op jit(solution)/shard_map/while/body/eval_jaxpr/shij,sihd->sjhd/dot_general | solution.py:68
  393.1 3.4 fusion.103
  396.6 6.2 %bitcast_dynamic-update-slice_fusion.4 = bf16[4,4,384,8,64]{2,4,3,1,0:T(8,128)(2,1)} fusion(bf16[4,4,384,8,64]{2,4,3,1,0:T(8,128)(2,1)} %get-tuple-element.211, s32[]{:T(128)} %get-tuple-element.210, f32[4,8,128,384]{3,2,1,0:T(8,128)} %copy-done.2, f32[4,8,128]{2,1,0:T(8,128)S(1)} %fusion.103, f32[4,8,128]{2,1,0:T(8,128)S(1)} %log_add_fusion.2, ...), kind=kOutput, calls=%fused_computation.14.clone.1 | convolution fusion | flops 414449664 | bytes 10521600 | tf_op jit(solution)/shard_map/while/body/eval_jaxpr/shij,sihd->sjhd/dot_general | solution.py:68
  402.7 4.0 fusion.54
  409.3 3.5 collective-permute-start.3
  412.8 88.9 %collective-permute-done.2 = bf16[2,16,128,512]{2,3,1,0:T(8,128)(2,1)S(1)} collective-permute-done((bf16[2,16,128,512]{2,3,1,0:T(8,128)(2,1)S(1)}, bf16[2,16,128,512]{2,3,1,0:T(8,128)(2,1)S(1)}, u32[]{:S(2)}, u32[]{:S(2)}) %collective-permute-start.2) | collective-permute-done | bytes 4194336 | tf_op jit(solution)/shard_map/ppermute | solution.py:27
  505.4 3.9 copy.40
  (74 shorter events, 50.2 us)
Async XLA Ops:
  0.6 198.7 %copy-start = (bf16[1024,512]{1,0:T(8,128)(2,1)S(1)}, bf16[1024,512]{1,0:T(8,128)(2,1)}, u32[]{:S(2)}) copy-start(bf16[1024,512]{1,0:T(8,128)(2,1)} %param.19) | copy-start | bytes 3145732
  2.8 13.7 %copy-start.8 = (bf16[24,1024]{1,0:T(8,128)(2,1)S(1)}, bf16[24,1024]{1,0:T(8,128)(2,1)}, u32[]{:S(2)}) copy-start(bf16[24,1024]{1,0:T(8,128)(2,1)} %param.15) | copy-start | bytes 147460
  2.8 17.5 %copy-start.9 = (f32[1024]{0:T(1024)S(1)}, f32[1024]{0:T(1024)}, u32[]{:S(2)}) copy-start(f32[1024]{0:T(1024)} %param.16) | copy-start | bytes 12292
  16.5 3.8 copy-start.3
  220.7 13.7 %copy-start.10 = (s32[16,3]{0,1:T(4,128)S(1)}, s32[16,3]{0,1:T(4,128)}, u32[]{:S(2)}) copy-start(s32[16,3]{0,1:T(4,128)} %param.22) | copy-start | bytes 580
  220.7 13.9 %copy-start.11 = (f32[8]{0:T(128)S(1)}, f32[8]{0:T(128)}, u32[]{:S(2)}) copy-start(f32[8]{0:T(128)} %param.21) | copy-start | bytes 100
  224.7 95.1 %collective-permute-start = (bf16[2,16,128,512]{2,3,1,0:T(8,128)(2,1)}, bf16[2,16,128,512]{2,3,1,0:T(8,128)(2,1)}, u32[]{:S(2)}, u32[]{:S(2)}) collective-permute-start(bf16[2,16,128,512]{2,3,1,0:T(8,128)(2,1)} %pad_maximum_fusion.2), channel_id=1, source_target_pairs={{0,1},{1,2},{2,3},{3,4},{4,5},{5,6},{6,7},{7,8},{8,9},{9,10},{10,1... | collective-permute-start | bytes 12582920 | tf_op jit(solution)/shard_map/ppermute | solution.py:18
  226.9 92.9 %collective-permute-start.1 = (bf16[2,16,128,512]{2,3,1,0:T(8,128)(2,1)}, bf16[2,16,128,512]{2,3,1,0:T(8,128)(2,1)}, u32[]{:S(2)}, u32[]{:S(2)}) collective-permute-start(bf16[2,16,128,512]{2,3,1,0:T(8,128)(2,1)} %pad_maximum_fusion.2), channel_id=1, source_target_pairs={{1,0},{2,1},{3,2},{4,3},{5,4},{6,5},{7,6},{8,7},{9,8},{10,9},{11,1... | collective-permute-start | bytes 12582920 | tf_op jit(solution)/shard_map/ppermute | solution.py:19
  326.1 6.0 %copy-start.6 = (bf16[4,4,128,8,64]{2,4,3,1,0:T(8,128)(2,1)S(1)}, bf16[4,4,128,8,64]{2,4,3,1,0:T(8,128)(2,1)}, u32[]{:S(2)}) copy-start(bf16[4,4,128,8,64]{2,4,3,1,0:T(8,128)(2,1)} %copy.39) | copy-start | bytes 6291460
  332.1 5.1 %copy-start.7 = (bf16[4,4,128,8,64]{2,4,3,1,0:T(8,128)(2,1)S(1)}, bf16[4,4,128,8,64]{2,4,3,1,0:T(8,128)(2,1)}, u32[]{:S(2)}) copy-start(bf16[4,4,128,8,64]{2,4,3,1,0:T(8,128)(2,1)} %get-tuple-element.226) | copy-start | bytes 6291460 | tf_op jit(solution)/shard_map/while
  334.9 5.2 %copy-start.2 = (f32[4,8,128,384]{3,2,1,0:T(8,128)}, f32[4,8,128,384]{3,2,1,0:T(8,128)S(1)}, u32[]{:S(2)}) copy-start(f32[4,8,128,384]{3,2,1,0:T(8,128)S(1)} %get-tuple-element.198) | copy-start | bytes 18874372 | tf_op jit(solution)/shard_map/while
  349.7 5.1 %copy-start.7 = (bf16[4,4,128,8,64]{2,4,3,1,0:T(8,128)(2,1)S(1)}, bf16[4,4,128,8,64]{2,4,3,1,0:T(8,128)(2,1)}, u32[]{:S(2)}) copy-start(bf16[4,4,128,8,64]{2,4,3,1,0:T(8,128)(2,1)} %get-tuple-element.226) | copy-start | bytes 6291460 | tf_op jit(solution)/shard_map/while
  352.5 5.2 %copy-start.2 = (f32[4,8,128,384]{3,2,1,0:T(8,128)}, f32[4,8,128,384]{3,2,1,0:T(8,128)S(1)}, u32[]{:S(2)}) copy-start(f32[4,8,128,384]{3,2,1,0:T(8,128)S(1)} %get-tuple-element.198) | copy-start | bytes 18874372 | tf_op jit(solution)/shard_map/while
  367.4 5.1 %copy-start.7 = (bf16[4,4,128,8,64]{2,4,3,1,0:T(8,128)(2,1)S(1)}, bf16[4,4,128,8,64]{2,4,3,1,0:T(8,128)(2,1)}, u32[]{:S(2)}) copy-start(bf16[4,4,128,8,64]{2,4,3,1,0:T(8,128)(2,1)} %get-tuple-element.226) | copy-start | bytes 6291460 | tf_op jit(solution)/shard_map/while
  370.2 5.2 %copy-start.2 = (f32[4,8,128,384]{3,2,1,0:T(8,128)}, f32[4,8,128,384]{3,2,1,0:T(8,128)S(1)}, u32[]{:S(2)}) copy-start(f32[4,8,128,384]{3,2,1,0:T(8,128)S(1)} %get-tuple-element.198) | copy-start | bytes 18874372 | tf_op jit(solution)/shard_map/while
  385.1 5.1 %copy-start.7 = (bf16[4,4,128,8,64]{2,4,3,1,0:T(8,128)(2,1)S(1)}, bf16[4,4,128,8,64]{2,4,3,1,0:T(8,128)(2,1)}, u32[]{:S(2)}) copy-start(bf16[4,4,128,8,64]{2,4,3,1,0:T(8,128)(2,1)} %get-tuple-element.226) | copy-start | bytes 6291460 | tf_op jit(solution)/shard_map/while
  387.9 5.2 %copy-start.2 = (f32[4,8,128,384]{3,2,1,0:T(8,128)}, f32[4,8,128,384]{3,2,1,0:T(8,128)S(1)}, u32[]{:S(2)}) copy-start(f32[4,8,128,384]{3,2,1,0:T(8,128)S(1)} %get-tuple-element.198) | copy-start | bytes 18874372 | tf_op jit(solution)/shard_map/while
  402.7 99.0 %copy-start.4 = (bf16[4,4,384,8,64]{2,4,3,1,0:T(8,128)(2,1)S(1)}, bf16[4,4,384,8,64]{2,4,3,1,0:T(8,128)(2,1)}, u32[]{:S(2)}) copy-start(bf16[4,4,384,8,64]{2,4,3,1,0:T(8,128)(2,1)} %get-tuple-element.50) | copy-start | bytes 18874372
  402.7 99.0 %copy-start.5 = (bf16[4,4,384,8,64]{2,4,3,1,0:T(8,128)(2,1)S(1)}, bf16[4,4,384,8,64]{2,4,3,1,0:T(8,128)(2,1)}, u32[]{:S(2)}) copy-start(bf16[4,4,384,8,64]{2,4,3,1,0:T(8,128)(2,1)} %get-tuple-element.51) | copy-start | bytes 18874372
  406.7 95.0 %collective-permute-start.2 = (bf16[2,16,128,512]{2,3,1,0:T(8,128)(2,1)S(1)}, bf16[2,16,128,512]{2,3,1,0:T(8,128)(2,1)S(1)}, u32[]{:S(2)}, u32[]{:S(2)}) collective-permute-start(bf16[2,16,128,512]{2,3,1,0:T(8,128)(2,1)S(1)} %get-tuple-element.135), channel_id=1, source_target_pairs={{0,1},{1,2},{2,3},{3,4},{4,5},{5,6},{6,7},{7,8},{8,9},{9,10},{10,1... | collective-permute-start | bytes 12582920 | tf_op jit(solution)/shard_map/ppermute | solution.py:27
  409.3 92.4 %collective-permute-start.3 = (bf16[2,16,128,512]{2,3,1,0:T(8,128)(2,1)S(1)}, bf16[2,16,128,512]{2,3,1,0:T(8,128)(2,1)S(1)}, u32[]{:S(2)}, u32[]{:S(2)}) collective-permute-start(bf16[2,16,128,512]{2,3,1,0:T(8,128)(2,1)S(1)} %get-tuple-element.136), channel_id=1, source_target_pairs={{1,0},{2,1},{3,2},{4,3},{5,4},{6,5},{7,6},{8,7},{9,8},{10,9},{11,1... | collective-permute-start | bytes 12582920 | tf_op jit(solution)/shard_map/ppermute | solution.py:27
  503.7 8.2 %copy-start.1 = (bf16[1024,512]{1,0:T(8,128)(2,1)S(1)}, bf16[1024,512]{1,0:T(8,128)(2,1)}, u32[]{:S(2)}) copy-start(bf16[1024,512]{1,0:T(8,128)(2,1)} %param.19) | copy-start | bytes 3145732
where the time goes:
time: 513 us; the launch traced here: 512 us
  waiting for transfers between devices  156 us (30%)
  local copies, waits for them, and re-layouts  103 us (20%)
  blocking collectives  98.4 us (19%)
  matrix products  82.8 us (16%)
  other arithmetic  58.4 us (11%)
  starting transfers between devices  11.9 us (2%)
    all_to_all x1, blocking collectives, on_device(): lax.all_to_all(normed, 'bus', split_axis=1, concat_axis=0, tiled=True)  98.4 us
    ppermute x2, waiting for transfers between devices, from_behind(): lax.ppermute(value, axis, [(source, source + steps) for source in range(l...  88.9 us
    ppermute x1, waiting for transfers between devices, with_halo(): before = lax.ppermute(last, axis, up)  66.6 us
    unnamed x27, local copies, waits for them, and re-layouts  39.7 us
    convert_element_type x1, local copies, waits for them, and re-layouts, on_device(): normed = (mixed * lax.rsqrt(jnp.mean(mixed * mixed, axis=-1, keepdims=Tru...  28.7 us
    unnamed x1, other arithmetic  25.9 us
    dot_general x4, matrix products, reader_terms(): jnp.einsum('shij,sihd->sjhd', dscores, queries, preferred_element_type=jn...  24.6 us
    dot_general x3, matrix products, on_device(): jnp.dot(flat_rows, weight, preferred_element_type=jnp.float32)  21.8 us
  transfers between devices with their start and end apart: 4, of which 2 were waited for; matrix products, arithmetic and copies ran while one was open for 4% of the time, Pallas kernels for 0%

commit v1 on v0

--- a/solution.py
+++ b/solution.py
@@ -6,6 +6,13 @@
 
 EPSILON = 1e-05
 NEG_FILL = -1e30
+
+
+def stacked_exchange(value, axis, split, join):
+    n_dev = lax.axis_size(axis)
+    blocks = jnp.stack(jnp.split(value, n_dev, axis=split), axis=0)
+    blocks = lax.all_to_all(blocks, axis, split_axis=0, concat_axis=0)
+    return jnp.concatenate(blocks, axis=join)
 
 
 def with_halo(shard, sides, width):
@@ -96,7 +103,7 @@
     normed = (
         mixed * lax.rsqrt(jnp.mean(mixed * mixed, axis=-1, keepdims=True) + EPSILON) * norm_gain
     ).astype(jnp.bfloat16)
-    arrived = lax.all_to_all(normed, "bus", split_axis=1, concat_axis=0, tiled=True)
+    arrived = stacked_exchange(normed, "bus", 1, 0)
     flat_rows = arrived.reshape(-1, arrived.shape[2])
     queries, key_rows, value_rows = [
         jnp.dot(flat_rows, weight, preferred_element_type=jnp.float32)

time: 513 us -> 432 us (0.84)
  local copies, waits for them, and re-layouts: 103 us -> 53.8 us
  other arithmetic: 58.4 us -> 32.4 us
  matrix products: 82.8 us -> 76.1 us
    convert_element_type x1 -> x0, local copies, waits for them, and re-layouts: 28.7 us -> none  [on_device(): normed = (mixed * lax.rsqrt(jnp.mean(mixed * mixed, axis=-1, keepdims=Tru...]
    unnamed x1 -> x2, other arithmetic: 25.9 us -> 0.01 us
    unnamed x27 -> x47, local copies, waits for them, and re-layouts: 39.7 us -> 15.9 us
    dot_general x3, matrix products: 21.8 us -> 15.7 us  [on_device(): jnp.dot(flat_rows, weight, preferred_element_type=jnp.float32)]
  transfers between devices with their start and end apart: 4 -> 4, of which waited for: 2 -> 2; matrix products, arithmetic and copies ran while one was open for 4% -> 5% of each run, Pallas kernels for 0% -> 0%
where the time goes in v1:
time: 432 us; the launch traced here: 431 us
  waiting for transfers between devices  157 us (36%)
  blocking collectives  98.1 us (23%)
  matrix products  76.1 us (18%)
  local copies, waits for them, and re-layouts  53.8 us (12%)
  other arithmetic  32.4 us (8%)
  starting transfers between devices  11.9 us (3%)
    all_to_all x1, blocking collectives, stacked_exchange(): blocks = lax.all_to_all(blocks, axis, split_axis=0, concat_axis=0)  98.1 us
    ppermute x2, waiting for transfers between devices, from_behind(): lax.ppermute(value, axis, [(source, source + steps) for source in range(l...  89 us
    ppermute x1, waiting for transfers between devices, with_halo(): before = lax.ppermute(last, axis, up)  67.7 us
    dot_general x4, matrix products, reader_terms(): jnp.einsum('shij,sihd->sjhd', dscores, queries, preferred_element_type=jn...  24.7 us
    unnamed x47, local copies, waits for them, and re-layouts  15.9 us
    dot_general x3, matrix products, on_device(): jnp.dot(flat_rows, weight, preferred_element_type=jnp.float32)  15.7 us
    dot_general x4, matrix products, reader_terms(): jnp.einsum('shij,sjhd->sihd', weights_b, value_tiles, preferred_element_t...  13.8 us
    gather x1, local copies, waits for them, and re-layouts, on_device(): ordered = jnp.take(series, bus_order, axis=1)  13.7 us
  transfers between devices with their start and end apart: 4, of which 2 were waited for; matrix products, arithmetic and copies ran while one was open for 5% of the time, Pallas kernels for 0%

profile of v1, /device:TPU:12, one launch (start us, length us, event | category | flops | bytes accessed | tf_op | source)
XLA Modules:
  0.0 430.9 jit_solution(9947494288320202125)
XLA Ops:
  2.8 13.7 %gather_fusion = bf16[2048,1024]{1,0:T(8,128)(2,1)} fusion(bf16[2048,1024]{1,0:T(8,128)(2,1)} %bitcast.180, s32[2048]{0:T(1024)S(1)} %fusion.72), kind=kCustom, calls=%fused_computation | custom fusion | bytes 8396800 | tf_op jit(solution)/shard_map/jit(_take)/gather | solution.py:97
  16.7 3.6 multiply_reduce_fusion
  22.4 98.1 %all_to_all.5 = bf16[16,1,128,1024]{3,2,1,0:T(8,128)(2,1)S(1)} all-to-all(bf16[16,1,128,1024]{3,2,1,0:T(8,128)(2,1)S(1)} %fusion.56), channel_id=1, replica_groups=mesh['grp'=2,'bus'=16] {'bus'}, dimensions={0} | all-to-all | bytes 8388608 | tf_op jit(solution)/shard_map/all_to_all | solution.py:14
  120.6 3.7 convolution_convert_fusion.2
  124.3 3.1 copy.19
  127.5 5.9 %convolution_convert_fusion.1 = bf16[2048,512]{1,0:T(8,128)(2,1)} fusion(bf16[2048,1024]{1,0:T(8,128)(2,1)} %bitcast.192, bf16[1024,512]{1,0:T(8,128)(2,1)S(1)} %copy-done.10), kind=kOutput, calls=%fused_computation.57 | convolution fusion | flops 2148532224 | bytes 7340032 | tf_op jit(solution)/shard_map/dot_general | solution.py:109
  133.3 3.9 copy.20
  137.2 3.9 pad_maximum_fusion.2
  143.5 3.5 collective-permute-start.1
  147.0 3.9 copy.21
  151.2 6.1 %convolution_convert_fusion.3 = bf16[2048,512]{1,0:T(8,128)(2,1)} fusion(bf16[2048,1024]{1,0:T(8,128)(2,1)} %bitcast.193, bf16[1024,512]{1,0:T(8,128)(2,1)} %param.18), kind=kOutput, calls=%fused_computation.59 | convolution fusion | flops 2148532224 | bytes 7340032 | tf_op jit(solution)/shard_map/dot_general | solution.py:109
  157.3 6.2 %reshape.213 = bf16[4,4,128,8,64]{4,3,2,1,0:T(8,128)(2,1)} reshape(bf16[2048,512]{1,0:T(8,128)(2,1)} %convolution_convert_fusion.3) | data formatting | bytes 4194304 | tf_op jit(solution)/shard_map/reshape;reshape;reshape | solution.py:44
  163.6 5.1 %copy.22 = bf16[4,4,128,8,64]{2,4,3,1,0:T(8,128)(2,1)} copy(bf16[4,4,128,8,64]{4,3,2,1,0:T(8,128)(2,1)} %reshape.213) | data formatting | bytes 4194304
  168.6 67.7 %collective-permute-done = bf16[2,16,128,512]{2,3,1,0:T(8,128)(2,1)} collective-permute-done((bf16[2,16,128,512]{2,3,1,0:T(8,128)(2,1)}, bf16[2,16,128,512]{2,3,1,0:T(8,128)(2,1)}, u32[]{:S(2)}, u32[]{:S(2)}) %collective-permute-start) | collective-permute-done | bytes 4194336 | tf_op jit(solution)/shard_map/ppermute | solution.py:25
  236.4 6.3 %pad_maximum_fusion = bf16[2,16,384,512]{2,3,1,0:T(8,128)(2,1)S(1)} fusion(bf16[2,16,128,512]{2,3,1,0:T(8,128)(2,1)} %collective-permute-done.1, bf16[1,16,128,512]{2,3,1,0:T(8,128)(2,1)} %copy.20, bf16[1,16,128,512]{2,3,1,0:T(8,128)(2,1)S(1)} %copy.19, bf16[2,16,128,512]{2,3,1,0:T(8,128)(2,1)} %collective-permute-done), kind=kLoop, calls=%fused_computation.47 | loop fusion | flops 50331648 | bytes 25165824 | tf_op jit(solution)/shard_map/concatenate | solution.py:27
  242.7 5.8 %fusion.79 = (bf16[1,16,384,512]{2,3,1,0:T(8,128)(2,1)}, bf16[1,16,384,512]{2,3,1,0:T(8,128)(2,1)}) fusion(bf16[2,16,384,512]{2,3,1,0:T(8,128)(2,1)S(1)} %pad_maximum_fusion), kind=kLoop, calls=%fused_computation.106 | loop fusion | bytes 25165824 | tf_op jit(solution)/shard_map/slice | solution.py:123
  248.5 73.1 %while.13 = (s32[]{:T(128)}, bf16[4,4,384,8,64]{2,4,3,1,0:T(8,128)(2,1)}, bf16[4,4,384,8,64]{2,4,3,1,0:T(8,128)(2,1)}, bf16[4,4,128,8,64]{2,4,3,1,0:T(8,128)(2,1...) while((s32[]{:T(128)}, ...), condition=%wide.region_4.5_spmd.clone, body=%wide.region_1.0_spmd.clone.sunk | while | flops 1044111360 | bytes 75687264 | solution.py:48
  254.3 2.8 bitcast_dynamic-update-slice_fusion.5
  257.1 3.4 fusion.104
  260.6 6.2 %bitcast_dynamic-update-slice_fusion.4 = bf16[4,4,384,8,64]{2,4,3,1,0:T(8,128)(2,1)} fusion(bf16[4,4,384,8,64]{2,4,3,1,0:T(8,128)(2,1)} %get-tuple-element.189, s32[]{:T(128)} %get-tuple-element.188, f32[4,8,128,384]{3,2,1,0:T(8,128)} %copy-done.2, f32[4,8,128]{2,1,0:T(8,128)S(1)} %fusion.104, f32[4,8,128]{2,1,0:T(8,128)S(1)} %log_add_fusion.2, ...), kind=kOutput, calls=%fused_computation.17.clone.1 | convolution fusion | flops 414449664 | bytes 10521600 | tf_op jit(solution)/shard_map/while/body/eval_jaxpr/shij,sihd->sjhd/dot_general | solution.py:75
  275.4 3.4 fusion.104
  278.8 6.2 %bitcast_dynamic-update-slice_fusion.4 = bf16[4,4,384,8,64]{2,4,3,1,0:T(8,128)(2,1)} fusion(bf16[4,4,384,8,64]{2,4,3,1,0:T(8,128)(2,1)} %get-tuple-element.189, s32[]{:T(128)} %get-tuple-element.188, f32[4,8,128,384]{3,2,1,0:T(8,128)} %copy-done.2, f32[4,8,128]{2,1,0:T(8,128)S(1)} %fusion.104, f32[4,8,128]{2,1,0:T(8,128)S(1)} %log_add_fusion.2, ...), kind=kOutput, calls=%fused_computation.17.clone.1 | convolution fusion | flops 414449664 | bytes 10521600 | tf_op jit(solution)/shard_map/while/body/eval_jaxpr/shij,sihd->sjhd/dot_general | solution.py:75
  290.8 2.8 bitcast_dynamic-update-slice_fusion.5
  293.7 3.4 fusion.104
  297.1 6.2 %bitcast_dynamic-update-slice_fusion.4 = bf16[4,4,384,8,64]{2,4,3,1,0:T(8,128)(2,1)} fusion(bf16[4,4,384,8,64]{2,4,3,1,0:T(8,128)(2,1)} %get-tuple-element.189, s32[]{:T(128)} %get-tuple-element.188, f32[4,8,128,384]{3,2,1,0:T(8,128)} %copy-done.2, f32[4,8,128]{2,1,0:T(8,128)S(1)} %fusion.104, f32[4,8,128]{2,1,0:T(8,128)S(1)} %log_add_fusion.2, ...), kind=kOutput, calls=%fused_computation.17.clone.1 | convolution fusion | flops 414449664 | bytes 10521600 | tf_op jit(solution)/shard_map/while/body/eval_jaxpr/shij,sihd->sjhd/dot_general | solution.py:75
  309.1 2.8 bitcast_dynamic-update-slice_fusion.5
  311.9 3.4 fusion.104
  315.4 6.2 %bitcast_dynamic-update-slice_fusion.4 = bf16[4,4,384,8,64]{2,4,3,1,0:T(8,128)(2,1)} fusion(bf16[4,4,384,8,64]{2,4,3,1,0:T(8,128)(2,1)} %get-tuple-element.189, s32[]{:T(128)} %get-tuple-element.188, f32[4,8,128,384]{3,2,1,0:T(8,128)} %copy-done.2, f32[4,8,128]{2,1,0:T(8,128)S(1)} %fusion.104, f32[4,8,128]{2,1,0:T(8,128)S(1)} %log_add_fusion.2, ...), kind=kOutput, calls=%fused_computation.17.clone.1 | convolution fusion | flops 414449664 | bytes 10521600 | tf_op jit(solution)/shard_map/while/body/eval_jaxpr/shij,sihd->sjhd/dot_general | solution.py:75
  321.6 4.0 fusion.54
  328.0 3.7 collective-permute-start.3
  331.7 89.0 %collective-permute-done.2 = bf16[2,16,128,512]{2,3,1,0:T(8,128)(2,1)S(1)} collective-permute-done((bf16[2,16,128,512]{2,3,1,0:T(8,128)(2,1)S(1)}, bf16[2,16,128,512]{2,3,1,0:T(8,128)(2,1)S(1)}, u32[]{:S(2)}, u32[]{:S(2)}) %collective-permute-start.2) | collective-permute-done | bytes 4194336 | tf_op jit(solution)/shard_map/ppermute | solution.py:34
  424.3 4.0 copy.24
  (95 shorter events, 40.8 us)
Async XLA Ops:
  0.6 120.0 %copy-start = (bf16[1024,512]{1,0:T(8,128)(2,1)S(1)}, bf16[1024,512]{1,0:T(8,128)(2,1)}, u32[]{:S(2)}) copy-start(bf16[1024,512]{1,0:T(8,128)(2,1)} %param.19) | copy-start | bytes 3145732
  2.8 13.8 %copy-start.7 = (bf16[24,1024]{1,0:T(8,128)(2,1)S(1)}, bf16[24,1024]{1,0:T(8,128)(2,1)}, u32[]{:S(2)}) copy-start(bf16[24,1024]{1,0:T(8,128)(2,1)} %param.15) | copy-start | bytes 147460
  16.5 3.7 copy-start.3
  16.5 3.7 copy-start.8
  120.6 3.7 copy-start.5
  124.3 3.1 copy-start.10
  141.1 9.8 %copy-start.9 = (s32[16,3]{0,1:T(4,128)S(1)}, s32[16,3]{0,1:T(4,128)}, u32[]{:S(2)}) copy-start(s32[16,3]{0,1:T(4,128)} %param.22) | copy-start | bytes 580
  141.1 10.0 %copy-start.11 = (f32[8]{0:T(128)S(1)}, f32[8]{0:T(128)}, u32[]{:S(2)}) copy-start(f32[8]{0:T(128)} %param.21) | copy-start | bytes 100
  141.1 95.2 %collective-permute-start = (bf16[2,16,128,512]{2,3,1,0:T(8,128)(2,1)}, bf16[2,16,128,512]{2,3,1,0:T(8,128)(2,1)}, u32[]{:S(2)}, u32[]{:S(2)}) collective-permute-start(bf16[2,16,128,512]{2,3,1,0:T(8,128)(2,1)} %pad_maximum_fusion.2), channel_id=1, source_target_pairs={{0,1},{1,2},{2,3},{3,4},{4,5},{5,6},{6,7},{7,8},{8,9},{9,10},{10,1... | collective-permute-start | bytes 12582920 | tf_op jit(solution)/shard_map/ppermute | solution.py:25
  143.5 92.9 %collective-permute-start.1 = (bf16[2,16,128,512]{2,3,1,0:T(8,128)(2,1)}, bf16[2,16,128,512]{2,3,1,0:T(8,128)(2,1)}, u32[]{:S(2)}, u32[]{:S(2)}) collective-permute-start(bf16[2,16,128,512]{2,3,1,0:T(8,128)(2,1)} %pad_maximum_fusion.2), channel_id=1, source_target_pairs={{1,0},{2,1},{3,2},{4,3},{5,4},{6,5},{7,6},{8,7},{9,8},{10,9},{11,1... | collective-permute-start | bytes 12582920 | tf_op jit(solution)/shard_map/ppermute | solution.py:26
  242.7 5.8 %copy-start.4 = (bf16[4,4,128,8,64]{2,4,3,1,0:T(8,128)(2,1)S(1)}, bf16[4,4,128,8,64]{2,4,3,1,0:T(8,128)(2,1)}, u32[]{:S(2)}) copy-start(bf16[4,4,128,8,64]{2,4,3,1,0:T(8,128)(2,1)} %copy.22) | copy-start | bytes 6291460
  251.2 5.9 %copy-start.2 = (f32[4,8,128,384]{3,2,1,0:T(8,128)}, f32[4,8,128,384]{3,2,1,0:T(8,128)S(1)}, u32[]{:S(2)}) copy-start(f32[4,8,128,384]{3,2,1,0:T(8,128)S(1)} %get-tuple-element.176) | copy-start | bytes 18874372 | tf_op jit(solution)/shard_map/while
  251.2 3.1 copy-start.6
  269.4 5.9 %copy-start.2 = (f32[4,8,128,384]{3,2,1,0:T(8,128)}, f32[4,8,128,384]{3,2,1,0:T(8,128)S(1)}, u32[]{:S(2)}) copy-start(f32[4,8,128,384]{3,2,1,0:T(8,128)S(1)} %get-tuple-element.176) | copy-start | bytes 18874372 | tf_op jit(solution)/shard_map/while
  269.4 3.1 copy-start.6
  287.7 6.0 %copy-start.2 = (f32[4,8,128,384]{3,2,1,0:T(8,128)}, f32[4,8,128,384]{3,2,1,0:T(8,128)S(1)}, u32[]{:S(2)}) copy-start(f32[4,8,128,384]{3,2,1,0:T(8,128)S(1)} %get-tuple-element.176) | copy-start | bytes 18874372 | tf_op jit(solution)/shard_map/while
  287.7 3.1 copy-start.6
  306.0 6.0 %copy-start.2 = (f32[4,8,128,384]{3,2,1,0:T(8,128)}, f32[4,8,128,384]{3,2,1,0:T(8,128)S(1)}, u32[]{:S(2)}) copy-start(f32[4,8,128,384]{3,2,1,0:T(8,128)S(1)} %get-tuple-element.176) | copy-start | bytes 18874372 | tf_op jit(solution)/shard_map/while
  306.0 3.1 copy-start.6
  321.6 99.1 %slice-start = ((s8[6291456]{0:T(1024)(128)(4,1)}), s8[4194304]{0:T(1024)(128)(4,1)S(1)}, s32[]{:S(2)}) async-start(s8[6291456]{0:T(1024)(128)(4,1)} %bitcast.183), calls=%async_computation.1 | async-start | bytes 8388608
  321.6 99.1 %slice-start.2 = ((s8[6291456]{0:T(1024)(128)(4,1)}), s8[4194304]{0:T(1024)(128)(4,1)S(1)}, s32[]{:S(2)}) async-start(s8[6291456]{0:T(1024)(128)(4,1)} %bitcast.187), calls=%async_computation.3 | async-start | bytes 8388608
  321.6 99.1 %slice-start.1 = ((s8[6291456]{0:T(1024)(128)(4,1)}), s8[2097152]{0:T(1024)(128)(4,1)S(1)}, s32[]{:S(2)}) async-start(s8[6291456]{0:T(1024)(128)(4,1)} %bitcast.183), calls=%async_computation.2 | async-start | bytes 4194304
  321.6 99.1 %slice-start.3 = ((s8[6291456]{0:T(1024)(128)(4,1)}), s8[2097152]{0:T(1024)(128)(4,1)S(1)}, s32[]{:S(2)}) async-start(s8[6291456]{0:T(1024)(128)(4,1)} %bitcast.187), calls=%async_computation.4 | async-start | bytes 4194304
  325.6 95.0 %collective-permute-start.2 = (bf16[2,16,128,512]{2,3,1,0:T(8,128)(2,1)S(1)}, bf16[2,16,128,512]{2,3,1,0:T(8,128)(2,1)S(1)}, u32[]{:S(2)}, u32[]{:S(2)}) collective-permute-start(bf16[2,16,128,512]{2,3,1,0:T(8,128)(2,1)S(1)} %get-tuple-element.113), channel_id=1, source_target_pairs={{0,1},{1,2},{2,3},{3,4},{4,5},{5,6},{6,7},{7,8},{8,9},{9,10},{10,1... | collective-permute-start | bytes 12582920 | tf_op jit(solution)/shard_map/ppermute | solution.py:34
  328.0 92.7 %collective-permute-start.3 = (bf16[2,16,128,512]{2,3,1,0:T(8,128)(2,1)S(1)}, bf16[2,16,128,512]{2,3,1,0:T(8,128)(2,1)S(1)}, u32[]{:S(2)}, u32[]{:S(2)}) collective-permute-start(bf16[2,16,128,512]{2,3,1,0:T(8,128)(2,1)S(1)} %get-tuple-element.114), channel_id=1, source_target_pairs={{1,0},{2,1},{3,2},{4,3},{5,4},{6,5},{7,6},{8,7},{9,8},{10,9},{11,1... | collective-permute-start | bytes 12582920 | tf_op jit(solution)/shard_map/ppermute | solution.py:34
  424.3 6.6 %copy-start.1 = (bf16[1024,512]{1,0:T(8,128)(2,1)S(1)}, bf16[1024,512]{1,0:T(8,128)(2,1)}, u32[]{:S(2)}) copy-start(bf16[1024,512]{1,0:T(8,128)(2,1)} %param.19) | copy-start | bytes 3145732
